TPU v7x, 128 devices: a whole 4x4x4 slice. The times are simulated.
128 devices in a mesh: elem: 8 (over y, core), bin: 16 (over z, x).
Axes of the slice: x: 4, y: 4, z: 4, core: 2. Of those that a mesh axis runs over, the one named last changes fastest.
Arguments:
- source: float32 [3, 128, 256, 128], P(None, 'elem', 'bin'), may hold values from -60 to 60
- viscosity: float32 [128, 256, 128], P('elem', 'bin'), may hold values from 0.3 to 3
- coarse_inverse: float32 [8, 128, 128], P('elem', 'bin'), may hold values from -0.06187184 to 2, as said below
- droplets: float32 [7, 8, 65536], P(None, 'elem', 'bin'), may hold values from -3 to 3, as said below
- droplet_elem: int32 [8, 65536], P('elem', 'bin'), may hold values from 0 to 63
- ghost_counts: int32 [2, 8, 16], P(None, 'elem', 'bin'), may hold values from 1 to 8, as said below
- tile_pairs: int32 [2, 8, 4096], P(None, 'elem', 'bin'), may hold values from 0 to 47, as said below
- tile_count: int32 [8, 16], P('elem', 'bin'), may hold values from 32 to 256, as said below
Outputs:
- velocity: float32 [3, 128, 256, 128], P(None, 'elem', 'bin')
- droplet_velocity: float32 [3, 8, 65536], P(None, 'elem', 'bin')
Inputs may be any that keep to these rules, and one draw needn't show every extreme that they name: `ghost_counts`: at least one bin sends 8 blocks to its lower neighbour and one to its upper neighbour. `tile_pairs`: row 0 names own blocks, below 32; row 1 names candidate blocks. `tile_count`: some bin uses all 256 tile slots. `droplets`: positions x, z and y lie in 0 to 1, diameters in 0.5 to 1.5. `coarse_inverse`: diagonal entries lie in 1 to 2.
All inputs are finite; a program needn't handle non-finite values.
Results may differ from a plain program's by a relative error of at most 0.0003.
Values sent between devices are 32-bit elements; how exact they have to be, the bound alone decides.
A program may use at most 128 MiB of HBM per device.

v0:
```python
import jax
import jax.numpy as jnp
import numpy as np
from jax import lax
from jax.sharding import PartitionSpec as P

ITERS = 4
NB = 32
BLOCK = 128
GMAX = 8
TGROUP = 16
PRECISE = lax.Precision.HIGHEST
MASS_TERM = 1.0
RELAXATION = 0.6
COARSE_GAIN = 0.02
SPREAD = 0.1
STIFFNESS = 0.3
TIME_STEP = 0.1


def extended(block, sides, width):
    for axis, dim in sides:
        count = lax.axis_size(axis)
        forward = [(i, i + 1) for i in range(count - 1)]
        forward.append((count - 1, 0))
        backward = [(target, source) for source, target in forward]
        low = lax.ppermute(
            lax.slice_in_dim(block, block.shape[dim] - width, None, axis=dim), axis, forward
        )
        high = lax.ppermute(lax.slice_in_dim(block, 0, width, axis=dim), axis, backward)
        block = jnp.concatenate([low, block, high], axis=dim)
    return block


def legendre_top(points):
    previous = points * 0.0 + 1.0
    current = points * 1.0
    for degree_index in range(1, 7):
        following = ((2 * degree_index + 1) * points * current - degree_index * previous) / (
            degree_index + 1
        )
        previous = current
        current = following
    return current


def gll_tables():
    points = np.array(
        [
            -1.0,
            -0.8717401485096066,
            -0.5917001814331423,
            -0.2092992179024789,
            0.2092992179024789,
            0.5917001814331423,
            0.8717401485096066,
            1.0,
        ]
    )
    weights = np.array(
        [
            0.03571428571428571,
            0.2107042271435061,
            0.3411226924835044,
            0.4124587946587038,
            0.4124587946587038,
            0.3411226924835044,
            0.2107042271435061,
            0.03571428571428571,
        ]
    )
    legendre = legendre_top(points)
    derivative = np.zeros((8, 8))
    for row_index in range(8):
        for col_index in range(8):
            if row_index != col_index:
                derivative[row_index, col_index] = (
                    legendre[row_index]
                    / legendre[col_index]
                    / (points[row_index] - points[col_index])
                )
    derivative[0, 0] = -14.0
    derivative[7, 7] = 14.0
    return (derivative.astype(np.float32), weights.astype(np.float32))


def seam_counts():
    return np.array([2.0, 1.0, 1.0, 1.0, 1.0, 1.0, 1.0, 2.0], np.float32)


def node_line(values, length):
    return jnp.asarray(np.tile(values, length // 8))


def nodal(line_x, line_y, line_z):
    return line_x[:, None, None] * line_y[None, :, None] * line_z[None, None, :]


def along(values, direction, matrix):
    amount = values.shape[direction] // 8
    divided = values.reshape(values.shape[:direction] + (amount, 8) + values.shape[direction + 1 :])
    contracted = jnp.tensordot(divided, matrix, axes=((direction + 1,), (1,)), precision=PRECISE)
    return jnp.moveaxis(contracted, -1, direction + 1).reshape(values.shape)


def seam_pass(values, direction, lower_plane, upper_plane):
    amount = values.shape[direction] // 8
    divided = values.reshape(values.shape[:direction] + (amount, 8) + values.shape[direction + 1 :])
    first_nodes = lax.index_in_dim(divided, 0, direction + 1, keepdims=False)
    last_nodes = lax.index_in_dim(divided, 7, direction + 1, keepdims=False)
    upper_sum = last_nodes + jnp.concatenate(
        [lax.slice_in_dim(first_nodes, 1, amount, axis=direction), upper_plane], direction
    )
    lower_sum = (
        jnp.concatenate(
            [lower_plane, lax.slice_in_dim(last_nodes, 0, amount - 1, axis=direction)], direction
        )
        + first_nodes
    )
    inner = lax.slice_in_dim(divided, 1, 7, axis=direction + 1)
    joined = jnp.concatenate(
        [
            jnp.expand_dims(lower_sum, direction + 1),
            inner,
            jnp.expand_dims(upper_sum, direction + 1),
        ],
        direction + 1,
    )
    return joined.reshape(values.shape)


def assemble(values):
    widened = extended(values, (("elem", 1), ("bin", 2)), 1)
    along_first = seam_pass(widened[:, 1:-1], 1, widened[:, :1], widened[:, -1:])
    along_second = seam_pass(
        along_first[:, :, 1:-1], 2, along_first[:, :, :1], along_first[:, :, -1:]
    )
    return seam_pass(along_second, 3, along_second[:, :, :, -1:], along_second[:, :, :, :1])


def prolong(coarse_cells):
    extent = coarse_cells.shape
    spread_cells = jnp.broadcast_to(
        coarse_cells[:, :, None, :, None, :, None],
        (extent[0], extent[1], 16, extent[2], 16, extent[3], 16),
    )
    return spread_cells.reshape(extent[0], extent[1] * 16, extent[2] * 16, extent[3] * 16)


def tile_force(candidates, own_block, cand_block, active):
    near_rows = candidates[own_block]
    far_rows = candidates[cand_block]
    distance = jnp.zeros((near_rows.shape[0], near_rows.shape[2], far_rows.shape[2]), jnp.float32)
    for component in range(3):
        offset = near_rows[:, component, :, None] - far_rows[:, component, None, :]
        distance = distance + offset * offset
    kernel = jnp.exp(-distance / SPREAD) * far_rows[:, 3, None, :] * active[:, None, None]
    summed = jnp.sum(kernel, axis=2)
    pulled = jnp.einsum("tab,tcb->tca", kernel, far_rows[:, :3], precision=PRECISE)
    return STIFFNESS * near_rows[:, 3, None, :] * (near_rows[:, :3] * summed[:, None, :] - pulled)


def collide_padded(candidates, tile_ids, limit):
    groups = tile_ids.shape[1] // TGROUP
    own_blocks = tile_ids[0].reshape(groups, TGROUP)
    cand_blocks = tile_ids[1].reshape(groups, TGROUP)
    positions = jnp.arange(groups * TGROUP, dtype=jnp.int32).reshape(groups, TGROUP)

    def advance(collision, entries):
        own_block, cand_block, position = entries
        active = (position < limit).astype(jnp.float32)
        return (
            collision.at[own_block].add(tile_force(candidates, own_block, cand_block, active)),
            None,
        )

    start_value = jnp.zeros((NB, 3, candidates.shape[2]), jnp.float32)
    collision, unused = lax.scan(advance, start_value, (own_blocks, cand_blocks, positions))
    return collision


def mask_size(part, kept):
    return jnp.concatenate([part[:3], part[3:] * kept[None, :]], 0)


def shift_height(part, amount):
    return jnp.concatenate([part[:1], part[1:2] + amount, part[2:]], 0)


def body(
    source, viscosity, coarse_inverse, droplets, droplet_elem, ghost_counts, tile_pairs, tile_count
):
    derivative, weights = gll_tables()
    deriv_table = jnp.asarray(derivative)
    square_table = deriv_table * deriv_table
    components, width_x, width_y, width_z = source.shape
    weight = nodal(
        node_line(weights, width_x), node_line(weights, width_y), node_line(weights, width_z)
    )
    multiplicity = nodal(
        node_line(seam_counts(), width_x),
        node_line(seam_counts(), width_y),
        node_line(seam_counts(), width_z),
    )
    coef_w = viscosity * weight
    identity = np.eye(width_z // 8, dtype=np.float32)
    forward_z = jnp.asarray(np.kron(identity, derivative.T))
    backward_z = jnp.asarray(np.kron(identity, derivative))
    square_z = jnp.asarray(np.kron(identity, derivative * derivative))

    def apply_local(component_field):
        summed = MASS_TERM * weight * component_field
        for direction in range(2):
            gradient = along(component_field, direction, deriv_table)
            summed = summed + along(coef_w * gradient, direction, deriv_table.T)
        gradient = jnp.dot(component_field, forward_z, precision=PRECISE)
        return summed + jnp.dot(coef_w * gradient, backward_z, precision=PRECISE)

    diagonal_local = MASS_TERM * weight
    for direction in range(2):
        diagonal_local = diagonal_local + along(coef_w, direction, square_table.T)
    diagonal_local = diagonal_local + jnp.dot(coef_w, square_z, precision=PRECISE)
    diag_sum = assemble(diagonal_local[None])[0]
    forcing = weight * source
    velocity = jnp.zeros_like(source)
    half_x, half_y, half_z = (width_x // 16, width_y // 16, width_z // 16)
    inverse_rows = coarse_inverse[0]
    for sweep_index in range(ITERS):
        if sweep_index == 0:
            residual = assemble(forcing)
        else:
            residual = assemble(
                forcing
                - jnp.stack([apply_local(velocity[component]) for component in range(components)])
            )
        coarse = (
            (weight * residual / multiplicity)
            .reshape(components, half_x, 16, half_y, 16, half_z, 16)
            .sum(axis=(2, 4, 6))
        )
        coarse = coarse.reshape(components, half_x * half_y * half_z)
        partial_dual = jnp.einsum("gh,cg->ch", inverse_rows, coarse, precision=PRECISE)
        coarse_dual = lax.psum(partial_dual, "bin")
        correction = jnp.einsum("gh,ch->cg", inverse_rows, coarse_dual, precision=PRECISE)
        correction = correction.reshape(components, half_x, half_y, half_z)
        velocity = velocity + assemble(
            (RELAXATION * residual / diag_sum + COARSE_GAIN * prolong(correction)) / multiplicity
        )
    element_mean = (weight * velocity).reshape(
        components, width_x // 8, 8, width_y // 8, 8, width_z // 8, 8
    ).sum(axis=(2, 4, 6)) / 8.0
    element_mean = element_mean.reshape(components, -1)
    own_drops = droplets[:, 0]
    position = jnp.stack([own_drops[0], own_drops[1], own_drops[2], own_drops[6]])
    span = GMAX * BLOCK
    block_ids = jnp.arange(span, dtype=jnp.int32) // BLOCK
    lower_count = ghost_counts[0, 0, 0]
    upper_count = ghost_counts[1, 0, 0]
    send_lower = mask_size(position[:, :span], (block_ids < lower_count).astype(jnp.float32))
    send_upper = mask_size(
        position[:, -span:], (block_ids >= GMAX - upper_count).astype(jnp.float32)
    )
    packet = jnp.concatenate([send_lower, send_upper], 1)
    widened = extended(packet, (("bin", 1),), span)
    from_below = shift_height(widened[:, :span], -1.0)
    from_above = shift_height(widened[:, -span:], 1.0)
    candidates = (
        jnp.concatenate([position, from_below, from_above], 1)
        .reshape(4, NB + 2 * GMAX, BLOCK)
        .transpose(1, 0, 2)
    )
    tile_ids = tile_pairs[:, 0]
    limit = tile_count[0, 0]
    collision = collide_padded(candidates, tile_ids, limit)
    collision = collision.transpose(1, 0, 2).reshape(3, own_drops.shape[1])
    element_ids = jnp.arange(element_mean.shape[1], dtype=jnp.int32)
    onehot = (droplet_elem[0][:, None] == element_ids[None, :]).astype(jnp.float32)
    sampled = jnp.einsum("ce,re->cr", element_mean, onehot, precision=PRECISE)
    speeds = own_drops[3:6]
    diameter = own_drops[6]
    updated = speeds + TIME_STEP * ((sampled - speeds) / (diameter * diameter) + collision)
    return (velocity, updated[:, None, :])


def solution(mesh):
    in_specs = (
        P(None, "elem", "bin", None),
        P("elem", "bin", None),
        P("elem", "bin", None),
        P(None, "elem", "bin"),
        P("elem", "bin"),
        P(None, "elem", "bin"),
        P(None, "elem", "bin"),
        P("elem", "bin"),
    )
    out_specs = (P(None, "elem", "bin", None), P(None, "elem", "bin"))
    return jax.shard_map(body, mesh=mesh, in_specs=in_specs, out_specs=out_specs, check_vma=False)
```

profile of v0, /device:TPU:0, one launch (start us, length us, event | category | flops | bytes accessed | tf_op | source)
XLA Modules:
  0.0 924.6 jit_solution(10439911834857078356)
XLA Ops:
  17.4 5.2 collective-permute-start.7
  39.1 5.9 collective-permute-start.3
  47.3 3.1 copy.1477
  53.7 3.1 copy.1454
  60.1 4.3 slice.1187
  67.9 3.4 fusion.126
  74.6 5.9 fusion.32
  80.6 5.3 copy.1461
  86.2 37.4 %psum.28 = f32[3,128]{1,0:T(4,128)S(1)} all-reduce(f32[3,128]{1,0:T(4,128)S(1)} %fusion.112), channel_id=1, replica_groups=mesh['elem'=8,'bin'=16] {'bin'}, use_global_device_ids=true, to_apply=%region_2.0 | all-reduce | flops 384 | bytes 3072 | tf_op jit(solution)/shard_map/psum | solution.py:243
  132.1 3.0 copy.1481
  139.1 5.2 collective-permute-start.11
  149.9 3.5 copy.1492
  156.3 4.2 slice.1233
  164.2 3.4 fusion.124
  171.8 3.3 pad_maximum_fusion.1
  177.9 3.1 copy.1500
  182.8 3.1 copy.1511
  189.9 3.1 copy.1522
  237.9 5.4 collective-permute-start.15
  246.5 3.1 copy.1538
  253.7 4.3 slice.1259
  261.1 3.5 fusion.123
  270.4 6.5 fusion.33
  276.9 5.2 copy.1544
  286.2 41.5 %psum.29 = f32[3,128]{1,0:T(4,128)} all-reduce(f32[3,128]{1,0:T(4,128)} %fusion.109), channel_id=1, replica_groups=mesh['elem'=8,'bin'=16] {'bin'}, use_global_device_ids=true, to_apply=%region_5.0 | all-reduce | flops 384 | bytes 3072 | tf_op jit(solution)/shard_map/psum | solution.py:243
  339.7 3.0 copy.1546
  347.2 5.3 collective-permute-start.19
  358.4 3.3 copy.1557
  364.6 4.2 slice.1282
  373.2 3.5 fusion.121
  380.6 4.7 maximum_add_fusion
  385.3 3.0 slice_bitcast_fusion.90
  388.9 3.1 copy.1565
  396.0 3.1 copy.1576
  403.1 3.1 copy.1587
  451.0 5.3 collective-permute-start.23
  457.0 5.3 collective-permute-start.37
  463.9 3.6 copy.1602
  469.6 4.3 slice.1308
  479.4 3.4 fusion.120
  488.3 6.5 fusion.34
  494.8 5.2 copy.1610
  504.1 37.3 %psum.30 = f32[3,128]{1,0:T(4,128)} all-reduce(f32[3,128]{1,0:T(4,128)} %fusion.106), channel_id=1, replica_groups=mesh['elem'=8,'bin'=16] {'bin'}, use_global_device_ids=true, to_apply=%region_8.0 | all-reduce | flops 384 | bytes 3072 | tf_op jit(solution)/shard_map/psum | solution.py:243
  553.2 3.0 copy.1612
  562.1 4.5 collective-permute-start.27
  574.4 3.3 copy.1623
  580.6 4.2 slice.1331
  589.2 3.5 fusion.118
  596.6 4.3 maximum_add_fusion.1
  600.9 3.1 slice_bitcast_fusion.87
  604.5 3.1 copy.1631
  611.6 3.1 copy.1642
  618.8 3.1 copy.1653
  666.8 5.3 collective-permute-start.31
  675.9 3.2 copy.1668
  681.2 4.3 slice.1357
  689.1 3.5 fusion.117
  696.0 6.0 fusion.35
  702.0 5.3 copy.1676
  707.5 40.4 %psum.31 = f32[3,128]{1,0:T(4,128)S(1)} all-reduce(f32[3,128]{1,0:T(4,128)S(1)} %fusion.103), channel_id=1, replica_groups=mesh['elem'=8,'bin'=16] {'bin'}, use_global_device_ids=true, to_apply=%region_11.12 | all-reduce | flops 384 | bytes 3072 | tf_op jit(solution)/shard_map/psum | solution.py:243
  759.3 5.3 collective-permute-start.35
  764.6 133.8 %while.10 = (s32[]{:T(128)}, f32[32,3,128]{2,1,0:T(4,128)S(1)}, s32[16,16]{1,0:T(8,128)}, f32[48,4,128]{2,1,0:T(4,128)S(1)}, s32[16,16]{1,0:T(8,128)}, /*index=5*/s32[16,16]{1,0:T(8,128)}, s32[]{:T(128)}, s32[]{:T(128)}) while((s32[]{:T(128)}, f32[32,3,128]{2,1,0:T(4,128)S(1)}, s32[16,16]{1,0:T(8,128)}, f32[48,4,128]{2,1,0:T(4,128)S(1)}, ...), condition=%wide.region_17.18_spmd, body=%wide.region_14.17_spmd.sunk | while | flops 16017570 | bytes 566241 | solution.py:178
  904.0 4.2 slice.1380
  912.4 6.3 multiply_reduce_fusion
  (814 shorter events, 517.6 us)
Async XLA Ops:
  0.6 85.4 %copy-start = (f32[1,8,128]{2,1,0:T(8,128)S(1)}, f32[1,8,128]{2,1,0:T(8,128)}, u32[]{:S(2)}) copy-start(f32[1,8,128]{2,1,0:T(8,128)} %param.22) | copy-start | bytes 12292
  0.6 22.0 %copy-start.46 = (f32[128]{0:T(128)S(1)}, f32[128]{0:T(128)}, u32[]{:S(2)}) copy-start(f32[128]{0:T(128)} %constant.85.clone) | copy-start | bytes 1540
  5.6 10.2 %collective-permute-start.4 = (f32[1,1,16,128]{3,2,1,0:T(8,128)S(1)}, f32[1,1,16,128]{3,2,1,0:T(8,128)S(1)}, u32[]{:S(2)}, u32[]{:S(2)}) collective-permute-start(f32[1,1,16,128]{3,2,1,0:T(8,128)S(1)} %get-tuple-element.284), channel_id=1, source_target_pairs={{0,16},{16,32},{32,48},{48,64},{64,80},{80,96},{96,112},{112,0},{1... | collective-permute-start | bytes 24584 | tf_op jit(solution)/shard_map/ppermute | solution.py:27
  5.6 10.2 %collective-permute-start.5 = (f32[1,1,16,128]{3,2,1,0:T(8,128)S(1)}, f32[1,1,16,128]{3,2,1,0:T(8,128)S(1)}, u32[]{:S(2)}, u32[]{:S(2)}) collective-permute-start(f32[1,1,16,128]{3,2,1,0:T(8,128)S(1)} %get-tuple-element.285), channel_id=1, source_target_pairs={{16,0},{32,16},{48,32},{64,48},{80,64},{96,80},{112,96},{0,112},{1... | collective-permute-start | bytes 24584 | tf_op jit(solution)/shard_map/ppermute | solution.py:30
  10.2 27.7 %collective-permute-start = (f32[3,1,16,128]{3,2,1,0:T(8,128)}, f32[3,1,16,128]{3,2,1,0:T(8,128)}, u32[]{:S(2)}, u32[]{:S(2)}) collective-permute-start(f32[3,1,16,128]{3,2,1,0:T(8,128)} %get-tuple-element.259), channel_id=1, source_target_pairs={{0,16},{16,32},{32,48},{48,64},{64,80},{80,96},{96,112},{112,0},{1... | collective-permute-start | bytes 73736 | tf_op jit(solution)/shard_map/ppermute | solution.py:27
  10.2 27.7 %collective-permute-start.1 = (f32[3,1,16,128]{3,2,1,0:T(8,128)}, f32[3,1,16,128]{3,2,1,0:T(8,128)}, u32[]{:S(2)}, u32[]{:S(2)}) collective-permute-start(f32[3,1,16,128]{3,2,1,0:T(8,128)} %get-tuple-element.260), channel_id=1, source_target_pairs={{16,0},{32,16},{48,32},{64,48},{80,64},{96,80},{112,96},{0,112},{1... | collective-permute-start | bytes 73736 | tf_op jit(solution)/shard_map/ppermute | solution.py:30
  15.8 8.1 collective-permute-start.6
  17.4 6.6 collective-permute-start.7
  39.1 11.4 %collective-permute-start.2 = (f32[3,18,1,128]{3,2,1,0:T(1,128)S(1)}, f32[3,18,1,128]{3,2,1,0:T(1,128)S(1)}, u32[]{:S(2)}, u32[]{:S(2)}) collective-permute-start(f32[3,18,1,128]{3,2,1,0:T(1,128)S(1)} %get-tuple-element.213), channel_id=1, source_target_pairs={{0,1},{1,2},{2,3},{3,4},{4,5},{5,6},{6,7},{7,8},{8,9},{9,10},{10,1... | collective-permute-start | bytes 82952 | tf_op jit(solution)/shard_map/ppermute | solution.py:27
  39.1 11.3 %collective-permute-start.3 = (f32[3,18,1,128]{3,2,1,0:T(1,128)S(1)}, f32[3,18,1,128]{3,2,1,0:T(1,128)S(1)}, u32[]{:S(2)}, u32[]{:S(2)}) collective-permute-start(f32[3,18,1,128]{3,2,1,0:T(1,128)S(1)} %get-tuple-element.214), channel_id=1, source_target_pairs={{1,0},{2,1},{3,2},{4,3},{5,4},{6,5},{7,6},{8,7},{9,8},{10,9},{11,1... | collective-permute-start | bytes 82952 | tf_op jit(solution)/shard_map/ppermute | solution.py:30
  129.2 6.6 collective-permute-start.8
  129.2 7.6 collective-permute-start.9
  137.8 9.7 %copy-start.12 = (f32[3,16,16,128]{3,2,1,0:T(8,128)S(1)}, f32[3,16,16,128]{3,2,1,0:T(8,128)}, u32[]{:S(2)}) copy-start(f32[3,16,16,128]{3,2,1,0:T(8,128)} %copy.1481) | copy-start | bytes 1179652
  139.0 7.2 collective-permute-start.10
  139.1 7.1 collective-permute-start.11
  198.4 14.9 %copy-start.20 = (f32[128,128,1]{1,0,2:T(8,128)S(1)}, f32[128,128,1]{1,0,2:T(8,128)}, u32[]{:S(2)}) copy-start(f32[128,128,1]{1,0,2:T(8,128)} %constant.101) | copy-start | bytes 196612
  213.3 15.7 %copy-start.19 = (f32[128,128,1]{1,0,2:T(8,128)S(1)}, f32[128,128,1]{1,0,2:T(8,128)}, u32[]{:S(2)}) copy-start(f32[128,128,1]{1,0,2:T(8,128)} %constant.102) | copy-start | bytes 196612
  225.0 7.9 copy-start.15
  233.2 4.5 collective-permute-start.12
  233.3 4.5 collective-permute-start.13
  237.8 7.2 collective-permute-start.14
  237.9 7.2 collective-permute-start.15
  330.6 8.4 copy-start.39
  336.1 6.6 collective-permute-start.16
  336.1 8.3 collective-permute-start.17
  346.0 10.0 %copy-start.11 = (f32[3,16,16,128]{3,2,1,0:T(8,128)S(1)}, f32[3,16,16,128]{3,2,1,0:T(8,128)}, u32[]{:S(2)}) copy-start(f32[3,16,16,128]{3,2,1,0:T(8,128)} %copy.1546) | copy-start | bytes 1179652
  346.0 10.0 %copy-start.30 = (f32[3,1,16,128]{3,2,1,0:T(8,128)S(1)}, f32[3,1,16,128]{3,2,1,0:T(8,128)}, u32[]{:S(2)}) copy-start(f32[3,1,16,128]{3,2,1,0:T(8,128)} %copy.1545) | copy-start | bytes 73732
  346.0 10.0 %copy-start.32 = (f32[3,1,16,128]{3,2,1,0:T(8,128)S(1)}, f32[3,1,16,128]{3,2,1,0:T(8,128)}, u32[]{:S(2)}) copy-start(f32[3,1,16,128]{3,2,1,0:T(8,128)} %copy.1547) | copy-start | bytes 73732
  347.1 7.5 collective-permute-start.18
  347.2 7.4 collective-permute-start.19
  438.4 7.9 copy-start.16
  438.4 11.0 %copy-start.40 = (f32[1,4096]{1,0:T(1,128)S(1)}, f32[1,4096]{1,0:T(1,128)}, u32[]{:S(2)}) copy-start(f32[1,4096]{1,0:T(1,128)} %get-tuple-element.287) | copy-start | bytes 49156
  438.4 18.0 %copy-start.33 = (f32[1,4096]{1,0:T(1,128)S(1)}, f32[1,4096]{1,0:T(1,128)}, u32[]{:S(2)}) copy-start(f32[1,4096]{1,0:T(1,128)} %get-tuple-element.288) | copy-start | bytes 49156
  438.4 18.0 %copy-start.35 = (f32[1,4096]{1,0:T(1,128)S(1)}, f32[1,4096]{1,0:T(1,128)}, u32[]{:S(2)}) copy-start(f32[1,4096]{1,0:T(1,128)} %get-tuple-element.289) | copy-start | bytes 49156
  438.4 18.0 %copy-start.37 = (f32[1,4096]{1,0:T(1,128)S(1)}, f32[1,4096]{1,0:T(1,128)}, u32[]{:S(2)}) copy-start(f32[1,4096]{1,0:T(1,128)} %get-tuple-element.290) | copy-start | bytes 49156
  446.4 4.5 collective-permute-start.20
  446.4 4.5 collective-permute-start.21
  450.9 11.4 %collective-permute-start.22 = (f32[3,18,1,128]{3,2,1,0:T(1,128)S(1)}, f32[3,18,1,128]{3,2,1,0:T(1,128)S(1)}, u32[]{:S(2)}, u32[]{:S(2)}) collective-permute-start(f32[3,18,1,128]{3,2,1,0:T(1,128)S(1)} %get-tuple-element.201), channel_id=1, source_target_pairs={{0,1},{1,2},{2,3},{3,4},{4,5},{5,6},{6,7},{7,8},{8,9},{9,10},{10,1... | collective-permute-start | bytes 82952 | tf_op jit(solution)/shard_map/ppermute | solution.py:27
  451.0 11.3 %collective-permute-start.23 = (f32[3,18,1,128]{3,2,1,0:T(1,128)S(1)}, f32[3,18,1,128]{3,2,1,0:T(1,128)S(1)}, u32[]{:S(2)}, u32[]{:S(2)}) collective-permute-start(f32[3,18,1,128]{3,2,1,0:T(1,128)S(1)} %get-tuple-element.202), channel_id=1, source_target_pairs={{1,0},{2,1},{3,2},{4,3},{5,4},{6,5},{7,6},{8,7},{9,8},{10,9},{11,1... | collective-permute-start | bytes 82952 | tf_op jit(solution)/shard_map/ppermute | solution.py:30
  457.0 208.2 %collective-permute-start.36 = (f32[4,1024]{1,0:T(4,128)}, f32[4,1024]{1,0:T(4,128)}, u32[]{:S(2)}, u32[]{:S(2)}) collective-permute-start(f32[4,1024]{1,0:T(4,128)} %get-tuple-element.291), channel_id=1, source_target_pairs={{0,1},{1,2},{2,3},{3,4},{4,5},{5,6},{6,7},{7,8},{8,9},{9,10},{10,1... | collective-permute-start | bytes 49160 | tf_op jit(solution)/shard_map/ppermute | solution.py:27
  457.0 215.1 %collective-permute-start.37 = (f32[4,1024]{1,0:T(4,128)}, f32[4,1024]{1,0:T(4,128)}, u32[]{:S(2)}, u32[]{:S(2)}) collective-permute-start(f32[4,1024]{1,0:T(4,128)} %get-tuple-element.292), channel_id=1, source_target_pairs={{1,0},{2,1},{3,2},{4,3},{5,4},{6,5},{7,6},{8,7},{9,8},{10,9},{11,1... | collective-permute-start | bytes 49160 | tf_op jit(solution)/shard_map/ppermute | solution.py:30
  469.6 5.5 copy-start.13
  544.3 8.3 copy-start.45
  549.7 6.6 collective-permute-start.24
  549.7 8.3 collective-permute-start.25
  561.3 8.6 collective-permute-start.26
  562.1 7.8 collective-permute-start.27
  654.0 7.9 copy-start.17
  662.2 4.5 collective-permute-start.28
  662.2 4.5 collective-permute-start.29
  666.7 7.7 collective-permute-start.30
  666.8 7.6 collective-permute-start.31
  701.9 46.2 %copy-start.3 = (f32[1,16,16,16,8]{2,4,3,1,0:T(8,128)S(1)}, f32[1,16,16,16,8]{2,4,3,1,0:T(8,128)}, u32[]{:S(2)}) copy-start(f32[1,16,16,16,8]{2,4,3,1,0:T(8,128)} %copy.1477) | copy-start | bytes 393220
  748.2 7.4 copy-start.34
  748.2 7.4 copy-start.36
  748.2 7.4 copy-start.38
  748.2 7.4 copy-start.41
  752.6 6.3 collective-permute-start.32
  752.7 6.4 collective-permute-start.33
  759.2 139.2 %collective-permute-start.34 = (f32[3,18,1,128]{3,2,1,0:T(1,128)S(1)}, f32[3,18,1,128]{3,2,1,0:T(1,128)S(1)}, u32[]{:S(2)}, u32[]{:S(2)}) collective-permute-start(f32[3,18,1,128]{3,2,1,0:T(1,128)S(1)} %get-tuple-element.193), channel_id=1, source_target_pairs={{0,1},{1,2},{2,3},{3,4},{4,5},{5,6},{6,7},{7,8},{8,9},{9,10},{10,1... | collective-permute-start | bytes 82952 | tf_op jit(solution)/shard_map/ppermute | solution.py:27
  759.3 139.1 %collective-permute-start.35 = (f32[3,18,1,128]{3,2,1,0:T(1,128)S(1)}, f32[3,18,1,128]{3,2,1,0:T(1,128)S(1)}, u32[]{:S(2)}, u32[]{:S(2)}) collective-permute-start(f32[3,18,1,128]{3,2,1,0:T(1,128)S(1)} %get-tuple-element.194), channel_id=1, source_target_pairs={{1,0},{2,1},{3,2},{4,3},{5,4},{6,5},{7,6},{8,7},{9,8},{10,9},{11,1... | collective-permute-start | bytes 82952 | tf_op jit(solution)/shard_map/ppermute | solution.py:30
  912.3 6.7 slice-start
  912.3 6.7 copy-start.44
  912.3 6.7 copy-start.47
  (23 other events, 67.4 us)
where the time goes:
time: 935 us; the launch traced here: 925 us
  local copies, waits for them, and re-layouts  342 us (37%)
  other arithmetic  209 us (22%)
  blocking collectives  157 us (17%)
  matrix products  120 us (13%)
  starting transfers between devices  82.7 us (9%)
    psum x4, blocking collectives, body(): coarse_dual = lax.psum(partial_dual, 'bin')  157 us
    ppermute x19, starting transfers between devices, extended(): lax.ppermute(lax.slice_in_dim(block, 0, width, axis=dim), axis, backward)  79.5 us
    dot_general x38, matrix products, along(): jnp.tensordot(divided, matrix, axes=((direction + 1,), (1,)), precision=P...  48.1 us
    dot_general x16, matrix products, tile_force(): jnp.einsum('tab,tcb->tca', kernel, far_rows[:, :3], precision=PRECISE)  41.6 us
    another operation x18, local copies, waits for them, and re-layouts, along(): values.reshape(values.shape[:direction] + (amount, 8) + values.shape[dire...  38.6 us
    slice x27, local copies, waits for them, and re-layouts, seam_pass(): inner = lax.slice_in_dim(divided, 1, 7, axis=direction + 1)  35.8 us
    concatenate x16, local copies, waits for them, and re-layouts, seam_pass(): jnp.concatenate([jnp.expand_dims(lower_sum, direction + 1), inner, jnp.ex...  33 us
    slice x10, other arithmetic, seam_pass(): last_nodes = lax.index_in_dim(divided, 7, direction + 1, keepdims=False)  29.1 us
  transfers between devices with their start and end apart: 38, of which 10 were waited for; matrix products, arithmetic and copies ran while one was open for 35% of the time, Pallas kernels for 0%

commit v1 on v0

--- a/solution.py
+++ b/solution.py
@@ -240,7 +240,11 @@
         )
         coarse = coarse.reshape(components, half_x * half_y * half_z)
         partial_dual = jnp.einsum("gh,cg->ch", inverse_rows, coarse, precision=PRECISE)
-        coarse_dual = lax.psum(partial_dual, "bin")
+        coarse_dual = partial_dual
+        for hop in (1, 2, 4, 8):
+            coarse_dual = coarse_dual + lax.ppermute(
+                coarse_dual, "bin", [(dev, dev ^ hop) for dev in range(16)]
+            )
         correction = jnp.einsum("gh,ch->cg", inverse_rows, coarse_dual, precision=PRECISE)
         correction = correction.reshape(components, half_x, half_y, half_z)
         velocity = velocity + assemble(

time: 935 us -> 823 us (0.88)
  blocking collectives: 157 us -> 0 us
  waiting for transfers between devices: 8.91 us -> 54.7 us
  other arithmetic: 209 us -> 186 us
  starting transfers between devices: 82.7 us -> 101 us
    psum x4 -> x0, blocking collectives: 157 us -> none  [body(): coarse_dual = lax.psum(partial_dual, 'bin')]
    ppermute x0 -> x16, waiting for transfers between devices: none -> 40.8 us  [body(): lax.ppermute(coarse_dual, 'bin', [(dev, dev ^ hop) for dev in range(16)])]
    ppermute x0 -> x16, starting transfers between devices: none -> 18.1 us  [body(): lax.ppermute(coarse_dual, 'bin', [(dev, dev ^ hop) for dev in range(16)])]
    select_n x16, other arithmetic: 11 us -> 0.2 us  [tile_force(): near_rows = candidates[own_block]]
    convert_element_type x16, other arithmetic: 21.3 us -> 10.5 us  [advance(): active = (position < limit).astype(jnp.float32)]
    unnamed x117 -> x119, local copies, waits for them, and re-layouts: 26.7 us -> 26.7 us
  transfers between devices with their start and end apart: 38 -> 54, of which waited for: 10 -> 24; matrix products, arithmetic and copies ran while one was open for 35% -> 25% of each run, Pallas kernels for 0% -> 0%
where the time goes in v1:
time: 823 us; the launch traced here: 809 us
  local copies, waits for them, and re-layouts  342 us (42%)
  other arithmetic  186 us (23%)
  matrix products  119 us (14%)
  starting transfers between devices  101 us (12%)
  waiting for transfers between devices  54.7 us (7%)
    ppermute x19, starting transfers between devices, extended(): lax.ppermute(lax.slice_in_dim(block, 0, width, axis=dim), axis, backward)  76.5 us
    dot_general x38, matrix products, along(): jnp.tensordot(divided, matrix, axes=((direction + 1,), (1,)), precision=P...  48.2 us
    dot_general x16, matrix products, tile_force(): jnp.einsum('tab,tcb->tca', kernel, far_rows[:, :3], precision=PRECISE)  41.6 us
    ppermute x16, waiting for transfers between devices, body(): lax.ppermute(coarse_dual, 'bin', [(dev, dev ^ hop) for dev in range(16)])  40.8 us
    another operation x18, local copies, waits for them, and re-layouts, along(): values.reshape(values.shape[:direction] + (amount, 8) + values.shape[dire...  38.7 us
    slice x27, local copies, waits for them, and re-layouts, seam_pass(): inner = lax.slice_in_dim(divided, 1, 7, axis=direction + 1)  35.8 us
    concatenate x16, local copies, waits for them, and re-layouts, seam_pass(): jnp.concatenate([jnp.expand_dims(lower_sum, direction + 1), inner, jnp.ex...  32.8 us
    slice x10, other arithmetic, seam_pass(): last_nodes = lax.index_in_dim(divided, 7, direction + 1, keepdims=False)  29.1 us
  transfers between devices with their start and end apart: 54, of which 24 were waited for; matrix products, arithmetic and copies ran while one was open for 25% of the time, Pallas kernels for 0%

profile of v1, /device:TPU:0, one launch (start us, length us, event | category | flops | bytes accessed | tf_op | source)
XLA Modules:
  0.0 808.7 jit_solution(1076017220118450317)
XLA Ops:
  17.5 5.2 collective-permute-start.7
  31.1 5.6 collective-permute-start.3
  44.1 3.2 copy.1454
  50.6 4.3 slice.1187
  59.0 3.5 fusion.130
  66.4 5.9 fusion.32
  86.9 14.0 %collective-permute-start.11 = (f32[3,128]{1,0:T(4,128)S(1)}, f32[3,128]{1,0:T(4,128)S(1)}, u32[]{:S(2)}, u32[]{:S(2)}) collective-permute-start(f32[3,128]{1,0:T(4,128)S(1)} %add.487), channel_id=1, source_target_pairs={{0,8},{1,9},{2,10},{3,11},{4,12},{5,13},{6,14},{7,15},{8,0},{9,1},... | collective-permute-start | bytes 4616 | tf_op jit(solution)/shard_map/ppermute | solution.py:245
  103.3 3.1 copy.1477
  106.4 5.3 copy.1461
  127.9 4.6 collective-permute-start.15
  138.1 3.1 copy.1492
  144.1 4.2 slice.1233
  152.0 3.5 fusion.128
  159.6 3.3 pad_maximum_fusion.1
  165.8 3.1 copy.1500
  170.7 3.1 copy.1511
  177.8 3.1 copy.1522
  226.0 5.4 collective-permute-start.19
  234.7 3.1 copy.1538
  241.8 4.3 slice.1259
  249.3 3.5 fusion.127
  258.6 6.5 fusion.33
  268.6 3.6 collective-permute-done.20
  272.3 5.0 collective-permute-done.21
  277.3 3.6 collective-permute-done.22
  282.8 5.2 copy.1544
  308.8 3.9 collective-permute-start.27
  318.4 3.3 copy.1557
  324.5 4.2 slice.1282
  333.1 3.5 fusion.125
  340.5 4.7 maximum_add_fusion
  348.8 3.1 copy.1565
  355.9 3.1 copy.1576
  411.0 5.3 collective-permute-start.31
  419.6 3.5 copy.1602
  425.3 4.3 slice.1308
  435.1 3.5 fusion.124
  443.9 6.5 fusion.34
  454.0 3.6 collective-permute-done.32
  458.8 3.8 collective-permute-done.33
  462.7 3.6 collective-permute-done.34
  468.2 5.3 copy.1610
  494.4 3.9 collective-permute-start.39
  504.1 3.3 copy.1623
  510.4 4.2 slice.1331
  518.9 3.4 fusion.122
  526.3 4.3 maximum_add_fusion.1
  534.2 3.1 copy.1631
  541.3 3.1 copy.1642
  548.5 3.1 copy.1653
  596.5 5.3 collective-permute-start.43
  602.0 5.3 collective-permute-start.53
  608.8 3.2 copy.1668
  614.2 4.3 slice.1357
  622.0 3.5 fusion.121
  628.9 6.0 fusion.35
  635.2 3.6 collective-permute-done.44
  639.0 4.9 collective-permute-done.45
  643.9 3.6 collective-permute-done.46
  647.5 5.4 copy.1676
  664.4 5.3 collective-permute-start.51
  669.7 112.7 %while.10 = (s32[]{:T(128)}, f32[32,3,128]{2,1,0:T(4,128)S(1)}, s32[16,16]{1,0:T(8,128)S(1)}, f32[48,4,128]{2,1,0:T(4,128)S(1)}, s32[16,16]{1,0:T(8,128)S(1)}, /*index=5*/s32[16,16]{1,0:T(8,128)S(1)}, s32[]{:T(128)}, s32[]{:T(128)}) while((s32[]{:T(128)}, f32[32,3,128]{2,1,0:T(4,128)S(1)}, s32[16,16]{1,0:T(8,128)S(1)}, ...), condition=%wide.region_13.14_spmd, body=%wide.region_10.13_spmd.sunk | while | flops 16017570 | bytes 566241 | solution.py:178
  788.0 4.1 slice.1380
  796.4 6.3 multiply_reduce_fusion
  (856 shorter events, 529.6 us)
Async XLA Ops:
  0.6 73.1 %copy-start = (f32[1,8,128]{2,1,0:T(8,128)S(1)}, f32[1,8,128]{2,1,0:T(8,128)}, u32[]{:S(2)}) copy-start(f32[1,8,128]{2,1,0:T(8,128)} %param.22) | copy-start | bytes 12292
  0.6 22.1 %copy-start.47 = (f32[128]{0:T(128)S(1)}, f32[128]{0:T(128)}, u32[]{:S(2)}) copy-start(f32[128]{0:T(128)} %constant.85.clone) | copy-start | bytes 1540
  5.5 10.2 %collective-permute-start.4 = (f32[1,1,16,128]{3,2,1,0:T(8,128)S(1)}, f32[1,1,16,128]{3,2,1,0:T(8,128)S(1)}, u32[]{:S(2)}, u32[]{:S(2)}) collective-permute-start(f32[1,1,16,128]{3,2,1,0:T(8,128)S(1)} %get-tuple-element.284), channel_id=1, source_target_pairs={{0,16},{16,32},{32,48},{48,64},{64,80},{80,96},{96,112},{112,0},{1... | collective-permute-start | bytes 24584 | tf_op jit(solution)/shard_map/ppermute | solution.py:27
  5.6 10.2 %collective-permute-start.5 = (f32[1,1,16,128]{3,2,1,0:T(8,128)S(1)}, f32[1,1,16,128]{3,2,1,0:T(8,128)S(1)}, u32[]{:S(2)}, u32[]{:S(2)}) collective-permute-start(f32[1,1,16,128]{3,2,1,0:T(8,128)S(1)} %get-tuple-element.285), channel_id=1, source_target_pairs={{16,0},{32,16},{48,32},{64,48},{80,64},{96,80},{112,96},{0,112},{1... | collective-permute-start | bytes 24584 | tf_op jit(solution)/shard_map/ppermute | solution.py:30
  10.2 19.1 %collective-permute-start = (f32[3,1,16,128]{3,2,1,0:T(8,128)}, f32[3,1,16,128]{3,2,1,0:T(8,128)}, u32[]{:S(2)}, u32[]{:S(2)}) collective-permute-start(f32[3,1,16,128]{3,2,1,0:T(8,128)} %get-tuple-element.259), channel_id=1, source_target_pairs={{0,16},{16,32},{32,48},{48,64},{64,80},{80,96},{96,112},{112,0},{1... | collective-permute-start | bytes 73736 | tf_op jit(solution)/shard_map/ppermute | solution.py:27
  10.2 19.1 %collective-permute-start.1 = (f32[3,1,16,128]{3,2,1,0:T(8,128)}, f32[3,1,16,128]{3,2,1,0:T(8,128)}, u32[]{:S(2)}, u32[]{:S(2)}) collective-permute-start(f32[3,1,16,128]{3,2,1,0:T(8,128)} %get-tuple-element.260), channel_id=1, source_target_pairs={{16,0},{32,16},{48,32},{64,48},{80,64},{96,80},{112,96},{0,112},{1... | collective-permute-start | bytes 73736 | tf_op jit(solution)/shard_map/ppermute | solution.py:30
  15.8 8.1 collective-permute-start.6
  17.5 6.6 collective-permute-start.7
  31.1 9.7 %collective-permute-start.2 = (f32[3,18,1,128]{3,2,1,0:T(1,128)}, f32[3,18,1,128]{3,2,1,0:T(1,128)}, u32[]{:S(2)}, u32[]{:S(2)}) collective-permute-start(f32[3,18,1,128]{3,2,1,0:T(1,128)} %get-tuple-element.213), channel_id=1, source_target_pairs={{0,1},{1,2},{2,3},{3,4},{4,5},{5,6},{6,7},{7,8},{8,9},{9,10},{10,1... | collective-permute-start | bytes 82952 | tf_op jit(solution)/shard_map/ppermute | solution.py:27
  31.1 9.7 %collective-permute-start.3 = (f32[3,18,1,128]{3,2,1,0:T(1,128)}, f32[3,18,1,128]{3,2,1,0:T(1,128)}, u32[]{:S(2)}, u32[]{:S(2)}) collective-permute-start(f32[3,18,1,128]{3,2,1,0:T(1,128)} %get-tuple-element.214), channel_id=1, source_target_pairs={{1,0},{2,1},{3,2},{4,3},{5,4},{6,5},{7,6},{8,7},{9,8},{10,9},{11,1... | collective-permute-start | bytes 82952 | tf_op jit(solution)/shard_map/ppermute | solution.py:30
  73.9 3.6 collective-permute-start.8
  77.5 5.2 collective-permute-start.9
  83.3 3.6 collective-permute-start.10
  86.9 24.7 %collective-permute-start.11 = (f32[3,128]{1,0:T(4,128)S(1)}, f32[3,128]{1,0:T(4,128)S(1)}, u32[]{:S(2)}, u32[]{:S(2)}) collective-permute-start(f32[3,128]{1,0:T(4,128)S(1)} %add.487), channel_id=1, source_target_pairs={{0,8},{1,9},{2,10},{3,11},{4,12},{5,13},{6,14},{7,15},{8,0},{9,1},... | collective-permute-start | bytes 4616 | tf_op jit(solution)/shard_map/ppermute | solution.py:245
  117.3 6.6 collective-permute-start.12
  117.3 7.6 collective-permute-start.13
  127.1 7.2 collective-permute-start.14
  127.9 6.4 collective-permute-start.15
  186.3 15.0 %copy-start.20 = (f32[128,128,1]{1,0,2:T(8,128)S(1)}, f32[128,128,1]{1,0,2:T(8,128)}, u32[]{:S(2)}) copy-start(f32[128,128,1]{1,0,2:T(8,128)} %constant.101) | copy-start | bytes 196612
  201.2 15.7 %copy-start.19 = (f32[128,128,1]{1,0,2:T(8,128)S(1)}, f32[128,128,1]{1,0,2:T(8,128)}, u32[]{:S(2)}) copy-start(f32[128,128,1]{1,0,2:T(8,128)} %constant.102) | copy-start | bytes 196612
  221.4 4.5 collective-permute-start.16
  221.4 4.5 collective-permute-start.17
  225.9 7.3 collective-permute-start.18
  226.0 7.2 collective-permute-start.19
  268.6 3.6 collective-permute-start.20
  272.2 5.1 collective-permute-start.21
  277.3 3.6 collective-permute-start.22
  281.5 6.5 collective-permute-start.23
  296.3 6.6 collective-permute-start.24
  296.3 8.2 %collective-permute-start.25 = (f32[3,1,16,128]{2,3,1,0:T(8,128)}, f32[3,1,16,128]{2,3,1,0:T(8,128)}, u32[]{:S(2)}, u32[]{:S(2)}) collective-permute-start(f32[3,1,16,128]{2,3,1,0:T(8,128)} %get-tuple-element.118), channel_id=1, source_target_pairs={{16,0},{32,16},{48,32},{64,48},{80,64},{96,80},{112,96},{0,112},{1... | collective-permute-start | bytes 73736 | tf_op jit(solution)/shard_map/ppermute | solution.py:30
  307.3 7.2 collective-permute-start.26
  308.8 5.8 collective-permute-start.27
  406.3 4.5 collective-permute-start.28
  406.3 4.5 collective-permute-start.29
  410.8 7.2 collective-permute-start.30
  411.0 7.0 collective-permute-start.31
  454.0 3.6 collective-permute-start.32
  457.6 5.1 collective-permute-start.33
  462.7 3.6 collective-permute-start.34
  466.8 6.7 collective-permute-start.35
  481.8 6.6 collective-permute-start.36
  481.8 8.3 %collective-permute-start.37 = (f32[3,1,16,128]{2,3,1,0:T(8,128)}, f32[3,1,16,128]{2,3,1,0:T(8,128)}, u32[]{:S(2)}, u32[]{:S(2)}) collective-permute-start(f32[3,1,16,128]{2,3,1,0:T(8,128)} %get-tuple-element.106), channel_id=1, source_target_pairs={{16,0},{32,16},{48,32},{64,48},{80,64},{96,80},{112,96},{0,112},{1... | collective-permute-start | bytes 73736 | tf_op jit(solution)/shard_map/ppermute | solution.py:30
  491.7 10.0 %copy-start.29 = (f32[3,1,16,128]{3,2,1,0:T(8,128)S(1)}, f32[3,1,16,128]{3,2,1,0:T(8,128)}, u32[]{:S(2)}) copy-start(f32[3,1,16,128]{3,2,1,0:T(8,128)} %copy.1611) | copy-start | bytes 73732
  491.7 10.0 %copy-start.30 = (f32[3,1,16,128]{3,2,1,0:T(8,128)S(1)}, f32[3,1,16,128]{3,2,1,0:T(8,128)}, u32[]{:S(2)}) copy-start(f32[3,1,16,128]{3,2,1,0:T(8,128)} %copy.1613) | copy-start | bytes 73732
  492.9 7.5 collective-permute-start.38
  494.4 6.0 collective-permute-start.39
  583.7 11.2 %copy-start.40 = (f32[1,4096]{1,0:T(1,128)S(1)}, f32[1,4096]{1,0:T(1,128)}, u32[]{:S(2)}) copy-start(f32[1,4096]{1,0:T(1,128)} %get-tuple-element.287) | copy-start | bytes 49156
  583.7 18.2 %copy-start.33 = (f32[1,4096]{1,0:T(1,128)S(1)}, f32[1,4096]{1,0:T(1,128)}, u32[]{:S(2)}) copy-start(f32[1,4096]{1,0:T(1,128)} %get-tuple-element.288) | copy-start | bytes 49156
  583.7 18.2 %copy-start.35 = (f32[1,4096]{1,0:T(1,128)S(1)}, f32[1,4096]{1,0:T(1,128)}, u32[]{:S(2)}) copy-start(f32[1,4096]{1,0:T(1,128)} %get-tuple-element.289) | copy-start | bytes 49156
  583.7 18.2 %copy-start.37 = (f32[1,4096]{1,0:T(1,128)S(1)}, f32[1,4096]{1,0:T(1,128)}, u32[]{:S(2)}) copy-start(f32[1,4096]{1,0:T(1,128)} %get-tuple-element.290) | copy-start | bytes 49156
  591.9 4.5 collective-permute-start.40
  591.9 4.5 collective-permute-start.41
  596.5 10.9 %collective-permute-start.42 = (f32[3,18,1,128]{3,2,1,0:T(1,128)S(1)}, f32[3,18,1,128]{3,2,1,0:T(1,128)S(1)}, u32[]{:S(2)}, u32[]{:S(2)}) collective-permute-start(f32[3,18,1,128]{3,2,1,0:T(1,128)S(1)} %get-tuple-element.195), channel_id=1, source_target_pairs={{0,1},{1,2},{2,3},{3,4},{4,5},{5,6},{6,7},{7,8},{8,9},{9,10},{10,1... | collective-permute-start | bytes 82952 | tf_op jit(solution)/shard_map/ppermute | solution.py:27
  596.5 10.8 %collective-permute-start.43 = (f32[3,18,1,128]{3,2,1,0:T(1,128)S(1)}, f32[3,18,1,128]{3,2,1,0:T(1,128)S(1)}, u32[]{:S(2)}, u32[]{:S(2)}) collective-permute-start(f32[3,18,1,128]{3,2,1,0:T(1,128)S(1)} %get-tuple-element.196), channel_id=1, source_target_pairs={{1,0},{2,1},{3,2},{4,3},{5,4},{6,5},{7,6},{8,7},{9,8},{10,9},{11,1... | collective-permute-start | bytes 82952 | tf_op jit(solution)/shard_map/ppermute | solution.py:30
  601.9 42.0 %collective-permute-start.52 = (f32[4,1024]{1,0:T(4,128)S(1)}, f32[4,1024]{1,0:T(4,128)S(1)}, u32[]{:S(2)}, u32[]{:S(2)}) collective-permute-start(f32[4,1024]{1,0:T(4,128)S(1)} %get-tuple-element.291), channel_id=1, source_target_pairs={{0,1},{1,2},{2,3},{3,4},{4,5},{5,6},{6,7},{7,8},{8,9},{9,10},{10,1... | collective-permute-start | bytes 49160 | tf_op jit(solution)/shard_map/ppermute | solution.py:27
  602.0 45.5 %collective-permute-start.53 = (f32[4,1024]{1,0:T(4,128)S(1)}, f32[4,1024]{1,0:T(4,128)S(1)}, u32[]{:S(2)}, u32[]{:S(2)}) collective-permute-start(f32[4,1024]{1,0:T(4,128)S(1)} %get-tuple-element.292), channel_id=1, source_target_pairs={{1,0},{2,1},{3,2},{4,3},{5,4},{6,5},{7,6},{8,7},{9,8},{10,9},{11,1... | collective-permute-start | bytes 49160 | tf_op jit(solution)/shard_map/ppermute | solution.py:30
  635.2 3.6 collective-permute-start.44
  638.8 5.1 collective-permute-start.45
  643.9 3.6 collective-permute-start.46
  647.5 5.5 collective-permute-start.47
  657.7 6.3 collective-permute-start.48
  657.7 6.4 collective-permute-start.49
  664.3 118.2 %collective-permute-start.50 = (f32[3,18,1,128]{3,2,1,0:T(1,128)S(1)}, f32[3,18,1,128]{3,2,1,0:T(1,128)S(1)}, u32[]{:S(2)}, u32[]{:S(2)}) collective-permute-start(f32[3,18,1,128]{3,2,1,0:T(1,128)S(1)} %get-tuple-element.193), channel_id=1, source_target_pairs={{0,1},{1,2},{2,3},{3,4},{4,5},{5,6},{6,7},{7,8},{8,9},{9,10},{10,1... | collective-permute-start | bytes 82952 | tf_op jit(solution)/shard_map/ppermute | solution.py:27
  664.4 118.1 %collective-permute-start.51 = (f32[3,18,1,128]{3,2,1,0:T(1,128)S(1)}, f32[3,18,1,128]{3,2,1,0:T(1,128)S(1)}, u32[]{:S(2)}, u32[]{:S(2)}) collective-permute-start(f32[3,18,1,128]{3,2,1,0:T(1,128)S(1)} %get-tuple-element.194), channel_id=1, source_target_pairs={{1,0},{2,1},{3,2},{4,3},{5,4},{6,5},{7,6},{8,7},{9,8},{10,9},{11,1... | collective-permute-start | bytes 82952 | tf_op jit(solution)/shard_map/ppermute | solution.py:30
  (40 other events, 215.8 us)
